TPU v7x, 32 devices: a whole 2x2x4 slice. The times are simulated.
32 devices in a mesh: blk: 4 (over x, core), ulysses: 8 (over z, y).
Axes of the slice: x: 2, y: 2, z: 4, core: 2. Of those that a mesh axis runs over, the one named last changes fastest.
Arguments:
- query_rows: bfloat16 [32, 4096, 128], P(None, ('blk', 'ulysses')), may hold values from -160 to 160
- out_grad: bfloat16 [32, 4096, 128], P(None, ('blk', 'ulysses')), may hold values from -6 to 6
- key_rows: bfloat16 [32, 512, 128], P(None, 'blk'), may hold values from -6 to 6
- value_rows: bfloat16 [32, 512, 128], P(None, 'blk'), may hold values from -6 to 6
- routes: int32 [4, 4], replicated, may hold values from 0 to 7
Outputs:
- query_grad: bfloat16 [32, 4096, 128], P(None, ('blk', 'ulysses'))
- key_grad: float32 [32, 512, 128], P(None, ('blk', 'ulysses'))
- value_grad: float32 [32, 512, 128], P(None, ('blk', 'ulysses'))
All inputs are finite; a program needn't handle non-finite values.
Results may differ from a plain program's by a relative error of at most 0.0056.
Values may be sent and summed in bfloat16 or wider, within the bound.
No kernel may reach another device: no remote copies, remote signals or barrier semaphores. Data moves between devices by JAX's collectives and lax.ppermute only.
A program may use at most 64 MiB of HBM per device.

v0:
```python
import math
import jax
import jax.numpy as jnp
from jax import lax
from jax.sharding import PartitionSpec as P

KB = 16


def body(query_rows, out_grad, key_rows, value_rows, routes):
    head_count, token_count, head_dim = query_rows.shape
    group_keys = key_rows.shape[1]
    cycle_size = lax.axis_size("blk")
    group_size = lax.axis_size("ulysses")
    sub_count = max(1, group_size // head_count)
    item_count = head_count * sub_count // group_size
    sub_length = token_count // sub_count
    row_count = group_size * sub_length
    block_count = group_keys // KB
    key_stride = token_count * group_size // group_keys
    score_scale = 1.0 / math.sqrt(head_dim)
    my_group = lax.axis_index("blk")
    my_rank = lax.axis_index("ulysses")
    packed_query = query_rows.reshape(head_count * sub_count, sub_length, head_dim)
    packed_grad = out_grad.reshape(head_count * sub_count, sub_length, head_dim)
    local_query, local_grad = (
        lax.all_to_all(packed_query, "ulysses", split_axis=0, concat_axis=1, tiled=True),
        lax.all_to_all(packed_grad, "ulysses", split_axis=0, concat_axis=1, tiled=True),
    )
    first_head = my_rank * item_count // sub_count
    own_keys = lax.dynamic_slice_in_dim(key_rows, first_head, item_count, 0)
    own_values = lax.dynamic_slice_in_dim(value_rows, first_head, item_count, 0)
    requested = lax.dynamic_index_in_dim(routes, my_group, 1, keepdims=False)
    block_ids = jnp.arange(block_count, dtype=jnp.int32)
    block_keys = own_keys.reshape(item_count, block_count, KB, head_dim)
    block_values = own_values.reshape(item_count, block_count, KB, head_dim)
    far_keys, far_values = (
        lax.all_to_all(
            jnp.take(block_keys, requested, axis=1), "blk", split_axis=1, concat_axis=1, tiled=True
        ),
        lax.all_to_all(
            jnp.take(block_values, requested, axis=1),
            "blk",
            split_axis=1,
            concat_axis=1,
            tiled=True,
        ),
    )
    near_keys = jnp.concatenate(
        [own_keys, far_keys.reshape(item_count, cycle_size * KB, head_dim)], axis=1
    )
    near_values = jnp.concatenate(
        [own_values, far_values.reshape(item_count, cycle_size * KB, head_dim)], axis=1
    )
    near_count = near_keys.shape[1]
    item_sub = (my_rank * item_count + jnp.arange(item_count, dtype=jnp.int32)) % sub_count
    far_visible = jnp.repeat(jnp.arange(cycle_size, dtype=jnp.int32) < my_group, KB)
    own_offsets = jnp.arange(group_keys, dtype=jnp.int32) * key_stride
    block_rows = 1024

    def attend(row_block, carried):
        query_out, key_acc, value_acc = carried
        row_start = row_block * block_rows
        queries = lax.dynamic_slice_in_dim(local_query, row_start, block_rows, 1)
        grad_rows = lax.dynamic_slice_in_dim(local_grad, row_start, block_rows, 1)
        row_ids = row_start + jnp.arange(block_rows, dtype=jnp.int32)
        positions = (
            row_ids[None, :] // sub_length * token_count
            + item_sub[:, None] * sub_length
            + row_ids[None, :] % sub_length
        )
        own_visible = own_offsets[None, None, :] <= positions[:, :, None]
        visible = jnp.concatenate(
            [
                own_visible,
                jnp.broadcast_to(far_visible, (item_count, block_rows, far_visible.shape[0])),
            ],
            axis=2,
        )
        scores = (
            jnp.einsum("ird,ikd->irk", queries, near_keys, preferred_element_type=jnp.float32)
            * score_scale
        )
        row_max = jnp.max(jnp.where(visible, scores, -jnp.inf), axis=-1, keepdims=True)
        expsum = jnp.where(visible, jnp.exp(scores - row_max), 0.0)
        weights = expsum / jnp.sum(expsum, axis=-1, keepdims=True)
        weights_half = weights.astype(jnp.bfloat16)
        attended = jnp.einsum(
            "irk,ikd->ird", weights_half, near_values, preferred_element_type=jnp.float32
        )
        delta_rows = jnp.sum(grad_rows.astype(jnp.float32) * attended, axis=-1, keepdims=True)
        dweights = jnp.einsum(
            "ird,ikd->irk", grad_rows, near_values, preferred_element_type=jnp.float32
        )
        dscore = (weights * (dweights - delta_rows)).astype(jnp.bfloat16)
        query_part = (
            jnp.einsum("irk,ikd->ird", dscore, near_keys, preferred_element_type=jnp.float32)
            * score_scale
        ).astype(jnp.bfloat16)
        key_acc = (
            key_acc
            + jnp.einsum("irk,ird->ikd", dscore, queries, preferred_element_type=jnp.float32)
            * score_scale
        )
        value_acc = value_acc + jnp.einsum(
            "irk,ird->ikd", weights_half, grad_rows, preferred_element_type=jnp.float32
        )
        query_out = lax.dynamic_update_slice_in_dim(query_out, query_part, row_start, 1)
        return (query_out, key_acc, value_acc)

    start_state = (
        jnp.zeros((item_count, row_count, head_dim), jnp.bfloat16),
        jnp.zeros((item_count, near_count, head_dim), jnp.float32),
        jnp.zeros((item_count, near_count, head_dim), jnp.float32),
    )
    query_out, key_acc, value_acc = lax.fori_loop(0, row_count // block_rows, attend, start_state)
    own_key_grad = key_acc[:, :group_keys]
    own_value_grad = value_acc[:, :group_keys]
    far_key_grad = key_acc[:, group_keys:].reshape(item_count, cycle_size, KB, head_dim)
    far_value_grad = value_acc[:, group_keys:].reshape(item_count, cycle_size, KB, head_dim)
    back_keys, back_values = (
        lax.all_to_all(far_key_grad, "blk", split_axis=1, concat_axis=1, tiled=True),
        lax.all_to_all(far_value_grad, "blk", split_axis=1, concat_axis=1, tiled=True),
    )
    placer = (requested[:, None] == block_ids[None, :]).astype(jnp.float32)
    added_keys = jnp.einsum(
        "gb,igkd->ibkd", placer, back_keys, precision=lax.Precision.HIGHEST
    ).reshape(item_count, group_keys, head_dim)
    added_values = jnp.einsum(
        "gb,igkd->ibkd", placer, back_values, precision=lax.Precision.HIGHEST
    ).reshape(item_count, group_keys, head_dim)
    key_share = (own_key_grad + added_keys).astype(jnp.bfloat16)
    value_share = (own_value_grad + added_values).astype(jnp.bfloat16)
    query_back, key_back, value_back = (
        lax.all_to_all(query_out, "ulysses", split_axis=1, concat_axis=0, tiled=True),
        lax.all_to_all(key_share, "ulysses", split_axis=1, concat_axis=0, tiled=True),
        lax.all_to_all(value_share, "ulysses", split_axis=1, concat_axis=0, tiled=True),
    )
    query_grad = query_back.reshape(head_count, token_count, head_dim)
    key_grad = jnp.sum(
        key_back.astype(jnp.float32).reshape(head_count, sub_count, -1, head_dim), axis=1
    )
    value_grad = jnp.sum(
        value_back.astype(jnp.float32).reshape(head_count, sub_count, -1, head_dim), axis=1
    )
    return (query_grad, key_grad, value_grad)


def solution(mesh):
    return jax.shard_map(
        body,
        mesh=mesh,
        in_specs=(
            P(None, ("blk", "ulysses"), None),
            P(None, ("blk", "ulysses"), None),
            P(None, "blk", None),
            P(None, "blk", None),
            P(),
        ),
        out_specs=(
            P(None, ("blk", "ulysses"), None),
            P(None, ("blk", "ulysses"), None),
            P(None, ("blk", "ulysses"), None),
        ),
        check_vma=False,
    )
```

profile of v0, /device:TPU:0, one launch (start us, length us, event | category | flops | bytes accessed | tf_op | source)
XLA Modules:
  0.0 155.4 jit_solution(3819428733041253633)
XLA Ops:
  0.6 0.0 copy-start
  0.7 0.7 copy-done
  1.3 0.2 dynamic-slice_reduce_fusion
  1.5 1.0 constant_dynamic-slice_fusion
  2.5 0.0 copy-start.5
  2.5 0.0 copy-start.3
  2.6 0.6 gather_fusion
  3.1 0.6 gather_fusion.1
  3.7 0.1 select_bitcast_fusion
  3.8 8.2 %all_to_all.92 = bf16[4,4,16,128]{3,2,0,1:T(8,128)(2,1)S(1)} all-to-all(bf16[4,4,16,128]{3,2,0,1:T(8,128)(2,1)S(1)} %get-tuple-element.29), channel_id=1, replica_groups=mesh['blk'=4,'ulysses'=8] {'blk'}, dimensions={1} | all-to-all | bytes 131072 | tf_op jit(solution)/shard_map/all_to_all | solution.py:38
  11.9 6.5 %all_to_all.93 = bf16[4,4,16,128]{3,2,0,1:T(8,128)(2,1)S(1)} all-to-all(bf16[4,4,16,128]{3,2,0,1:T(8,128)(2,1)S(1)} %get-tuple-element.28), channel_id=1, replica_groups=mesh['blk'=4,'ulysses'=8] {'blk'}, dimensions={1} | all-to-all | bytes 131072 | tf_op jit(solution)/shard_map/all_to_all | solution.py:41
  18.4 31.4 %all_to_all.94 = bf16[32,128,128]{2,1,0:T(8,128)(2,1)S(1)} all-to-all(bf16[32,128,128]{2,1,0:T(8,128)(2,1)} %param.7), channel_id=1, replica_groups=mesh['blk'=4,'ulysses'=8] {'ulysses'}, dimensions={0} | all-to-all | bytes 2097152 | tf_op jit(solution)/shard_map/all_to_all | solution.py:27
  49.8 3.6 %all-to-all-start.3 = ((bf16[32,128,128]{2,1,0:T(8,128)(2,1)}), bf16[32,128,128]{2,1,0:T(8,128)(2,1)S(1)}, u32[]{:S(2)}, u32[]{:S(2)}) async-start(bf16[32,128,128]{2,1,0:T(8,128)(2,1)} %param.8), calls=%async_computation.3 | async-start | bytes 2097152 | tf_op jit(solution)/shard_map/all_to_all | solution.py:28
  53.4 0.1 broadcast_in_dim.43
  53.5 0.1 reshape.186
  53.6 1.0 broadcast_compare_fusion
  54.6 0.0 copy-start.7
  54.6 0.6 copy.32
  55.3 0.0 copy-done.5
  55.3 0.1 copy.31
  55.4 23.6 %all-to-all-done.3 = bf16[32,128,128]{2,1,0:T(8,128)(2,1)S(1)} async-done(((bf16[32,128,128]{2,1,0:T(8,128)(2,1)}), bf16[32,128,128]{2,1,0:T(8,128)(2,1)S(1)}, u32[]{:S(2)}, u32[]{:S(2)}) %all-to-all-start.3) | async-done | bytes 1048608 | tf_op jit(solution)/shard_map/all_to_all | solution.py:28
  79.0 1.0 copy.33
  80.0 0.0 copy-done.3
  80.0 4.5 %fusion.40 = (f32[4,1024]{1,0:T(4,128)S(1)}, f32[4,1024,192]{1,2,0:T(8,128)}) fusion(pred[4,1024,128]{1,2,0:T(32,128)(4,1)} %broadcast_compare_fusion, pred[192]{0:T(512)(128)(4,1)S(1)} %pad.5.clone, bf16[4,1024,128]{2,1,0:T(8,128)(2,1)S(1)} %bitcast.73, bf16[4,64,128]{2,1,0:T(8,128)(2,1)S(1)} %bitcast.90, bf16[4,128,128]{2,1,0:T(8,128)(2,1)S(1)} %get-tuple-element.33), kind=kOutput, calls=%fused_computation.69 | convolution fusion | flops 409731264 | bytes 4931776 | tf_op jit(solution)/shard_map/while/body/eval_jaxpr/sub | solution.py:85
  84.5 0.0 copy-done.7
  84.5 0.0 copy-start.1
  84.5 0.0 copy-start.6
  84.5 0.0 copy-start.9
  84.6 2.4 %fusion.8 = bf16[4,1024,192]{1,2,0:T(8,128)(2,1)S(1)} fusion(f32[4,1024,192]{1,2,0:T(8,128)} %get-tuple-element.31, f32[4,1024]{1,0:T(4,128)S(1)} %get-tuple-element.30), kind=kLoop, calls=%fused_computation.17 | loop fusion | flops 1572864 | bytes 4734976 | tf_op jit(solution)/shard_map/while/body/eval_jaxpr/convert_element_type | solution.py:87
  87.0 0.0 copy-done.1
  87.0 0.6 fusion.41
  87.6 0.7 copy.42
  88.2 3.3 %all-to-all-start.7 = ((f32[4,4,16,128]{3,2,0,1:T(8,128)}), f32[4,4,16,128]{3,2,0,1:T(8,128)S(1)}, u32[]{:S(2)}, u32[]{:S(2)}) async-start(f32[4,4,16,128]{3,2,0,1:T(8,128)} %copy.42), calls=%async_computation.7 | async-start | bytes 262144 | tf_op jit(solution)/shard_map/all_to_all | solution.py:123
  91.6 0.0 copy-start.2
  91.6 0.0 copy-done.6
  91.6 0.0 copy-done.9
  91.6 2.5 %multiply_reduce_fusion = f32[4,1024]{1,0:T(4,128)S(1)} fusion(bf16[4,1024,128]{2,1,0:T(8,128)(2,1)} %bitcast.75, bf16[4,1024,192]{1,2,0:T(8,128)(2,1)S(1)} %fusion.8, bf16[4,64,128]{2,1,0:T(8,128)(2,1)S(1)} %bitcast.92, bf16[4,128,128]{2,1,0:T(8,128)(2,1)S(1)} %copy-done.6), kind=kOutput, calls=%fused_computation.12 | convolution fusion | flops 203288576 | bytes 2834432 | tf_op jit(solution)/shard_map/while/body/eval_jaxpr/irk,ikd->ird/dot_general | solution.py:88
  94.1 0.0 copy-done.2
  94.1 2.5 %fusion.1 = bf16[4,1024,192]{1,2,0:T(8,128)(2,1)S(1)} fusion(bf16[4,1024,128]{2,1,0:T(8,128)(2,1)S(1)} %bitcast.77, f32[4,1024]{1,0:T(4,128)S(1)} %multiply_reduce_fusion, f32[4,1024,192]{1,2,0:T(8,128)} %get-tuple-element.31, f32[4,1024]{1,0:T(4,128)S(1)} %get-tuple-element.30, bf16[4,64,128]{2,1,0:T(8,128)(2,1)S(1)} %bitcast.93, ...), kind=kOutput, calls=%fused_computation.4 | convolution fusion | flops 204865536 | bytes 5996544 | tf_op jit(solution)/shard_map/while/body/eval_jaxpr/ird,ikd->irk/dot_general | solution.py:92
  96.6 0.6 convolution_multiply_fusion
  97.2 0.0 copy-start.4
  97.2 0.0 copy-start.8
  97.2 0.7 copy.37
  97.9 0.0 all-to-all-done.7
  97.9 3.3 %all-to-all-start.5 = ((f32[4,4,16,128]{3,2,0,1:T(8,128)}), f32[4,4,16,128]{3,2,0,1:T(8,128)S(1)}, u32[]{:S(2)}, u32[]{:S(2)}) async-start(f32[4,4,16,128]{3,2,0,1:T(8,128)} %copy.37), calls=%async_computation.5 | async-start | bytes 262144 | tf_op jit(solution)/shard_map/all_to_all | solution.py:122
  101.2 0.4 convolution_bitcast_fusion
  101.7 0.8 copy.45
  102.5 3.3 %all-to-all-done.5 = f32[4,4,16,128]{3,2,0,1:T(8,128)S(1)} async-done(((f32[4,4,16,128]{3,2,0,1:T(8,128)}), f32[4,4,16,128]{3,2,0,1:T(8,128)S(1)}, u32[]{:S(2)}, u32[]{:S(2)}) %all-to-all-start.5) | async-done | bytes 131104 | tf_op jit(solution)/shard_map/all_to_all | solution.py:122
  105.8 3.4 %all-to-all-start.8 = ((bf16[4,128,128]{2,0,1:T(4,128)(2,1)}), bf16[4,128,128]{2,0,1:T(4,128)(2,1)S(1)}, u32[]{:S(2)}, u32[]{:S(2)}) async-start(bf16[4,128,128]{2,0,1:T(4,128)(2,1)} %copy.45), calls=%async_computation.8 | async-start | bytes 262144 | tf_op jit(solution)/shard_map/all_to_all | solution.py:137
  109.2 0.4 convolution_bitcast_fusion.1
  109.7 0.8 copy.40
  110.5 6.1 %all-to-all-done.8 = bf16[4,128,128]{2,0,1:T(4,128)(2,1)S(1)} async-done(((bf16[4,128,128]{2,0,1:T(4,128)(2,1)}), bf16[4,128,128]{2,0,1:T(4,128)(2,1)S(1)}, u32[]{:S(2)}, u32[]{:S(2)}) %all-to-all-start.8) | async-done | bytes 131104 | tf_op jit(solution)/shard_map/all_to_all | solution.py:137
  116.6 3.4 %all-to-all-start.6 = ((bf16[4,128,128]{2,0,1:T(4,128)(2,1)}), bf16[4,128,128]{2,0,1:T(4,128)(2,1)S(1)}, u32[]{:S(2)}, u32[]{:S(2)}) async-start(bf16[4,128,128]{2,0,1:T(4,128)(2,1)} %copy.40), calls=%async_computation.6 | async-start | bytes 262144 | tf_op jit(solution)/shard_map/all_to_all | solution.py:136
  120.0 0.0 copy-done.4
  120.0 0.0 copy-done.8
  120.0 1.0 multiply_convert_fusion
  120.9 1.8 %copy.35 = bf16[4,1024,128]{2,0,1:T(4,128)(2,1)} copy(bf16[4,1024,128]{2,1,0:T(8,128)(2,1)S(1)} %multiply_convert_fusion) | data formatting | bytes 2097152 | tf_op jit(solution)/shard_map/while/body/eval_jaxpr/convert_element_type | solution.py:99
  122.7 4.5 %all-to-all-done.6 = bf16[4,128,128]{2,0,1:T(4,128)(2,1)S(1)} async-done(((bf16[4,128,128]{2,0,1:T(4,128)(2,1)}), bf16[4,128,128]{2,0,1:T(4,128)(2,1)S(1)}, u32[]{:S(2)}, u32[]{:S(2)}) %all-to-all-start.6) | async-done | bytes 131104 | tf_op jit(solution)/shard_map/all_to_all | solution.py:136
  127.2 3.6 %all-to-all-start.4 = ((bf16[4,1024,128]{2,0,1:T(4,128)(2,1)}), bf16[4,1024,128]{2,0,1:T(4,128)(2,1)S(1)}, u32[]{:S(2)}, u32[]{:S(2)}) async-start(bf16[4,1024,128]{2,0,1:T(4,128)(2,1)} %copy.35), calls=%async_computation.4 | async-start | bytes 2097152 | tf_op jit(solution)/shard_map/all_to_all | solution.py:135
  130.8 0.7 copy.46
  131.6 0.7 copy.41
  132.3 21.9 %all-to-all-done.4 = bf16[4,1024,128]{2,0,1:T(4,128)(2,1)S(1)} async-done(((bf16[4,1024,128]{2,0,1:T(4,128)(2,1)}), bf16[4,1024,128]{2,0,1:T(4,128)(2,1)S(1)}, u32[]{:S(2)}, u32[]{:S(2)}) %all-to-all-start.4) | async-done | bytes 1048608 | tf_op jit(solution)/shard_map/all_to_all | solution.py:135
  154.2 1.2 copy.36
  (16 shorter events, 0.3 us)
Async XLA Ops:
  0.6 0.7 copy-start
  2.5 52.8 %copy-start.5 = (bf16[4,128,128]{2,1,0:T(8,128)(2,1)}, bf16[4,128,128]{2,1,0:T(8,128)(2,1)S(1)}, u32[]{:S(2)}) copy-start(bf16[4,128,128]{2,1,0:T(8,128)(2,1)S(1)} %get-tuple-element.32) | copy-start | bytes 393220
  2.5 77.5 %copy-start.3 = (bf16[4,128,128]{2,1,0:T(8,128)(2,1)}, bf16[4,128,128]{2,1,0:T(8,128)(2,1)S(1)}, u32[]{:S(2)}) copy-start(bf16[4,128,128]{2,1,0:T(8,128)(2,1)S(1)} %get-tuple-element.33) | copy-start | bytes 393220
  49.8 29.2 %all-to-all-start.3 = ((bf16[32,128,128]{2,1,0:T(8,128)(2,1)}), bf16[32,128,128]{2,1,0:T(8,128)(2,1)S(1)}, u32[]{:S(2)}, u32[]{:S(2)}) async-start(bf16[32,128,128]{2,1,0:T(8,128)(2,1)} %param.8), calls=%async_computation.3 | async-start | bytes 2097152 | tf_op jit(solution)/shard_map/all_to_all | solution.py:28
  54.6 29.9 %copy-start.7 = (bf16[4,4,16,128]{3,2,1,0:T(8,128)(2,1)}, bf16[4,4,16,128]{3,2,1,0:T(8,128)(2,1)S(1)}, u32[]{:S(2)}) copy-start(bf16[4,4,16,128]{3,2,1,0:T(8,128)(2,1)S(1)} %copy.30) | copy-start | bytes 196612
  84.5 2.5 %copy-start.1 = (bf16[8,4,128,128]{3,2,0,1:T(8,128)(2,1)S(1)}, bf16[8,4,128,128]{3,2,0,1:T(8,128)(2,1)}, u32[]{:S(2)}) copy-start(bf16[8,4,128,128]{3,2,0,1:T(8,128)(2,1)} %copy.33) | copy-start | bytes 3145732
  84.5 7.1 %copy-start.6 = (bf16[4,128,128]{2,1,0:T(8,128)(2,1)S(1)}, bf16[4,128,128]{2,1,0:T(8,128)(2,1)}, u32[]{:S(2)}) copy-start(bf16[4,128,128]{2,1,0:T(8,128)(2,1)} %copy-done.5) | copy-start | bytes 393220
  84.5 7.1 %copy-start.9 = (bf16[4,4,16,128]{3,2,1,0:T(8,128)(2,1)S(1)}, bf16[4,4,16,128]{3,2,1,0:T(8,128)(2,1)}, u32[]{:S(2)}) copy-start(bf16[4,4,16,128]{3,2,1,0:T(8,128)(2,1)} %copy.32) | copy-start | bytes 196612
  88.2 9.6 %all-to-all-start.7 = ((f32[4,4,16,128]{3,2,0,1:T(8,128)}), f32[4,4,16,128]{3,2,0,1:T(8,128)S(1)}, u32[]{:S(2)}, u32[]{:S(2)}) async-start(f32[4,4,16,128]{3,2,0,1:T(8,128)} %copy.42), calls=%async_computation.7 | async-start | bytes 262144 | tf_op jit(solution)/shard_map/all_to_all | solution.py:123
  91.6 2.5 %copy-start.2 = (bf16[8,4,128,128]{3,2,0,1:T(8,128)(2,1)S(1)}, bf16[8,4,128,128]{3,2,0,1:T(8,128)(2,1)}, u32[]{:S(2)}) copy-start(bf16[8,4,128,128]{3,2,0,1:T(8,128)(2,1)} %copy.33) | copy-start | bytes 3145732
  97.2 22.8 %copy-start.4 = (bf16[4,128,128]{2,1,0:T(8,128)(2,1)S(1)}, bf16[4,128,128]{2,1,0:T(8,128)(2,1)}, u32[]{:S(2)}) copy-start(bf16[4,128,128]{2,1,0:T(8,128)(2,1)} %copy-done.3) | copy-start | bytes 393220
  97.2 22.8 %copy-start.8 = (bf16[4,4,16,128]{3,2,1,0:T(8,128)(2,1)S(1)}, bf16[4,4,16,128]{3,2,1,0:T(8,128)(2,1)}, u32[]{:S(2)}) copy-start(bf16[4,4,16,128]{3,2,1,0:T(8,128)(2,1)} %copy-done.7) | copy-start | bytes 196612
  97.9 7.9 %all-to-all-start.5 = ((f32[4,4,16,128]{3,2,0,1:T(8,128)}), f32[4,4,16,128]{3,2,0,1:T(8,128)S(1)}, u32[]{:S(2)}, u32[]{:S(2)}) async-start(f32[4,4,16,128]{3,2,0,1:T(8,128)} %copy.37), calls=%async_computation.5 | async-start | bytes 262144 | tf_op jit(solution)/shard_map/all_to_all | solution.py:122
  105.8 10.8 %all-to-all-start.8 = ((bf16[4,128,128]{2,0,1:T(4,128)(2,1)}), bf16[4,128,128]{2,0,1:T(4,128)(2,1)S(1)}, u32[]{:S(2)}, u32[]{:S(2)}) async-start(bf16[4,128,128]{2,0,1:T(4,128)(2,1)} %copy.45), calls=%async_computation.8 | async-start | bytes 262144 | tf_op jit(solution)/shard_map/all_to_all | solution.py:137
  116.6 10.7 %all-to-all-start.6 = ((bf16[4,128,128]{2,0,1:T(4,128)(2,1)}), bf16[4,128,128]{2,0,1:T(4,128)(2,1)S(1)}, u32[]{:S(2)}, u32[]{:S(2)}) async-start(bf16[4,128,128]{2,0,1:T(4,128)(2,1)} %copy.40), calls=%async_computation.6 | async-start | bytes 262144 | tf_op jit(solution)/shard_map/all_to_all | solution.py:136
  127.2 26.9 %all-to-all-start.4 = ((bf16[4,1024,128]{2,0,1:T(4,128)(2,1)}), bf16[4,1024,128]{2,0,1:T(4,128)(2,1)S(1)}, u32[]{:S(2)}, u32[]{:S(2)}) async-start(bf16[4,1024,128]{2,0,1:T(4,128)(2,1)} %copy.35), calls=%async_computation.4 | async-start | bytes 2097152 | tf_op jit(solution)/shard_map/all_to_all | solution.py:135
where the time goes:
time: 156 us; the launch traced here: 155 us
  waiting for transfers between devices  59.4 us (38%)
  blocking collectives  46 us (29%)
  starting transfers between devices  20.6 us (13%)
  local copies, waits for them, and re-layouts  12.4 us (8%)
  matrix products  12.4 us (8%)
  other arithmetic  3.66 us (2%)
    all_to_all x1, blocking collectives, body(): lax.all_to_all(packed_query, 'ulysses', split_axis=0, concat_axis=1, tile...  31.4 us
    all_to_all x1, waiting for transfers between devices, body(): lax.all_to_all(packed_grad, 'ulysses', split_axis=0, concat_axis=1, tiled...  23.6 us
    all_to_all x1, waiting for transfers between devices, body(): lax.all_to_all(query_out, 'ulysses', split_axis=1, concat_axis=0, tiled=T...  21.9 us
    all_to_all x1, blocking collectives, body(): lax.all_to_all(jnp.take(block_keys, requested, axis=1), 'blk', split_axis...  8.16 us
    all_to_all x1, blocking collectives, body(): lax.all_to_all(jnp.take(block_values, requested, axis=1), 'blk', split_ax...  6.47 us
    all_to_all x1, waiting for transfers between devices, body(): lax.all_to_all(value_share, 'ulysses', split_axis=1, concat_axis=0, tiled...  6.08 us
    all_to_all x1, waiting for transfers between devices, body(): lax.all_to_all(key_share, 'ulysses', split_axis=1, concat_axis=0, tiled=T...  4.52 us
    sub x1, matrix products, attend(): expsum = jnp.where(visible, jnp.exp(scores - row_max), 0.0)  4.49 us
  transfers between devices with their start and end apart: 6, of which 5 were waited for; matrix products, arithmetic and copies ran while one was open for 10% of the time, Pallas kernels for 0%

commit v1 on v0

--- a/solution.py
+++ b/solution.py
@@ -7,7 +7,39 @@
 KB = 16
 
 
+def perform_the_ports(w_in, in_dim, my_data):
+    d_next, tmp = (w_in.shape[:in_dim], w_in.shape[in_dim + 1 :])
+    tall = w_in.reshape(*d_next, my_data, -1, *tmp)
+    val = jnp.moveaxis(tall, in_dim, 0)
+    return val
+
+
+def direct_results(shard_in, pos_dim):
+    state_now = list(shard_in.shape[1:])
+    state_now[pos_dim] *= shard_in.shape[0]
+    built = jnp.moveaxis(shard_in, 0, pos_dim).reshape(state_now)
+    return built
+
+
 def body(query_rows, out_grad, key_rows, value_rows, routes):
+
+    def define_sites_up(view, mesh_dim, unit, chunk):
+        odd = lax.axis_size(mesh_dim)
+        f_now = lax.axis_index(mesh_dim)
+        s_next, plain = (odd, f_now)
+        arr_next = perform_the_ports(view, unit, s_next)
+        leaves = [arr_next[plain]]
+        for it in range(1, s_next):
+            formed = arr_next[plain ^ it]
+            t_next = lax.ppermute(
+                formed, axis_name=mesh_dim, perm=[(q, q ^ it) for q in range(s_next)]
+            )
+            leaves.append(t_next)
+        lower = jnp.stack(leaves)
+        arr_next = lower[plain ^ jnp.arange(s_next)]
+        block_now = direct_results(arr_next, chunk)
+        return block_now
+
     head_count, token_count, head_dim = query_rows.shape
     group_keys = key_rows.shape[1]
     cycle_size = lax.axis_size("blk")
@@ -24,7 +56,7 @@
     packed_query = query_rows.reshape(head_count * sub_count, sub_length, head_dim)
     packed_grad = out_grad.reshape(head_count * sub_count, sub_length, head_dim)
     local_query, local_grad = (
-        lax.all_to_all(packed_query, "ulysses", split_axis=0, concat_axis=1, tiled=True),
+        define_sites_up(packed_query, "ulysses", 0, 1),
         lax.all_to_all(packed_grad, "ulysses", split_axis=0, concat_axis=1, tiled=True),
     )
     first_head = my_rank * item_count // sub_count

time: 156 us -> 149 us (0.955)
  blocking collectives: 46 us -> 0 us
  starting transfers between devices: 20.6 us -> 51.5 us
  local copies, waits for them, and re-layouts: 12.4 us -> 17 us
  waiting for transfers between devices: 59.4 us -> 62.8 us
    all_to_all x3 -> x0, blocking collectives: 46 us -> none  [the longest x1 31.4 us: body(): lax.all_to_all(packed_query, 'ulysses', split_axis=0, concat_axis=1, tile...]
    all_to_all x1, waiting for transfers between devices: 23.6 us -> 0.01 us  [body(): lax.all_to_all(packed_grad, 'ulysses', split_axis=0, concat_axis=1, tiled...]
    ppermute x0 -> x7, waiting for transfers between devices: none -> 21.2 us  [define_sites_up(): lax.ppermute(formed, axis_name=mesh_dim, perm=[(q, q ^ it) for q in range...]
    ppermute x0 -> x7, starting transfers between devices: none -> 14.3 us  [define_sites_up(): lax.ppermute(formed, axis_name=mesh_dim, perm=[(q, q ^ it) for q in range...]
    all_to_all x1, starting transfers between devices: 3.44 us -> 12.2 us  [body(): lax.all_to_all(value_share, 'ulysses', split_axis=1, concat_axis=0, tiled...]
    all_to_all x0 -> x2, starting transfers between devices: none -> 6.57 us  [the longest x1 3.29 us: body(): lax.all_to_all(jnp.take(block_values, requested, axis=1), 'blk', split_ax...]
    all_to_all x0 -> x2, waiting for transfers between devices: none -> 5.93 us  [the longest x1 3.83 us: body(): lax.all_to_all(jnp.take(block_keys, requested, axis=1), 'blk', split_axis...]
  transfers between devices with their start and end apart: 6 -> 15, of which waited for: 5 -> 8; matrix products, arithmetic and copies ran while one was open for 10% -> 18% of each run, Pallas kernels for 0% -> 0%
where the time goes in v1:
time: 149 us; the launch traced here: 148 us
  waiting for transfers between devices  62.8 us (42%)
  starting transfers between devices  51.5 us (35%)
  local copies, waits for them, and re-layouts  17 us (11%)
  matrix products  12.1 us (8%)
  other arithmetic  3.41 us (2%)
    all_to_all x1, waiting for transfers between devices, body(): lax.all_to_all(query_out, 'ulysses', split_axis=1, concat_axis=0, tiled=T...  21.7 us
    ppermute x7, waiting for transfers between devices, define_sites_up(): lax.ppermute(formed, axis_name=mesh_dim, perm=[(q, q ^ it) for q in range...  21.2 us
    ppermute x7, starting transfers between devices, define_sites_up(): lax.ppermute(formed, axis_name=mesh_dim, perm=[(q, q ^ it) for q in range...  14.3 us
    all_to_all x1, starting transfers between devices, body(): lax.all_to_all(value_share, 'ulysses', split_axis=1, concat_axis=0, tiled...  12.2 us
    all_to_all x1, waiting for transfers between devices, body(): lax.all_to_all(value_share, 'ulysses', split_axis=1, concat_axis=0, tiled...  6.08 us
    all_to_all x1, starting transfers between devices, body(): lax.all_to_all(packed_grad, 'ulysses', split_axis=0, concat_axis=1, tiled...  4.88 us
    all_to_all x1, waiting for transfers between devices, body(): lax.all_to_all(key_share, 'ulysses', split_axis=1, concat_axis=0, tiled=T...  4.52 us
    sub x1, matrix products, attend(): expsum = jnp.where(visible, jnp.exp(scores - row_max), 0.0)  4.22 us
  transfers between devices with their start and end apart: 15, of which 8 were waited for; matrix products, arithmetic and copies ran while one was open for 18% of the time, Pallas kernels for 0%

profile of v1, /device:TPU:0, one launch (start us, length us, event | category | flops | bytes accessed | tf_op | source)
XLA Modules:
  0.0 147.9 jit_solution(3814734142644426341)
XLA Ops:
  0.6 0.0 copy-start
  0.7 1.4 dynamic-slice_bitcast_fusion
  2.1 3.1 %collective-permute-start = (bf16[4,128,128]{2,1,0:T(8,128)(2,1)S(1)}, bf16[4,128,128]{2,1,0:T(8,128)(2,1)S(1)}, u32[]{:S(2)}, u32[]{:S(2)}) collective-permute-start(bf16[4,128,128]{2,1,0:T(8,128)(2,1)S(1)} %get-tuple-element.34), channel_id=1, source_target_pairs={{0,1},{1,0},{2,3},{3,2},{4,5},{5,4},{6,7},{7,6},{8,9},{9,8},{10,11... | collective-permute-start | bytes 393224 | tf_op jit(solution)/shard_map/ppermute | solution.py:34
  5.1 1.6 %collective-permute-start.1 = (bf16[4,128,128]{2,1,0:T(8,128)(2,1)S(1)}, bf16[4,128,128]{2,1,0:T(8,128)(2,1)S(1)}, u32[]{:S(2)}, u32[]{:S(2)}) collective-permute-start(bf16[4,128,128]{2,1,0:T(8,128)(2,1)S(1)} %get-tuple-element.33), channel_id=1, source_target_pairs={{0,2},{1,3},{2,0},{3,1},{4,6},{5,7},{6,4},{7,5},{8,10},{9,11},{10,... | collective-permute-start | bytes 393224 | tf_op jit(solution)/shard_map/ppermute | solution.py:34
  6.7 0.0 collective-permute-start.2
  6.7 3.0 %collective-permute-start.3 = (bf16[4,128,128]{2,1,0:T(8,128)(2,1)S(1)}, bf16[4,128,128]{2,1,0:T(8,128)(2,1)S(1)}, u32[]{:S(2)}, u32[]{:S(2)}) collective-permute-start(bf16[4,128,128]{2,1,0:T(8,128)(2,1)S(1)} %get-tuple-element.31), channel_id=1, source_target_pairs={{0,4},{1,5},{2,6},{3,7},{4,0},{5,1},{6,2},{7,3},{8,12},{9,13},{10,... | collective-permute-start | bytes 393224 | tf_op jit(solution)/shard_map/ppermute | solution.py:34
  9.7 1.3 collective-permute-start.4
  11.0 0.2 fusion.26
  11.2 1.0 constant_dynamic-slice_fusion
  12.2 0.0 copy-start.3
  12.2 0.6 gather_fusion.1
  12.8 0.6 gather_fusion.2
  13.3 0.7 select_bitcast_fusion
  14.1 3.3 %all-to-all-start = ((bf16[4,4,16,128]{3,2,0,1:T(8,128)(2,1)}), bf16[4,4,16,128]{3,2,0,1:T(8,128)(2,1)S(1)}, u32[]{:S(2)}, u32[]{:S(2)}) async-start(bf16[4,4,16,128]{3,2,0,1:T(8,128)(2,1)} %get-tuple-element.49), calls=%async_computation | async-start | bytes 131072 | tf_op jit(solution)/shard_map/all_to_all | solution.py:70
  17.4 0.2 broadcast_compare_fusion
  17.6 3.8 %all-to-all-done = bf16[4,4,16,128]{3,2,0,1:T(8,128)(2,1)S(1)} async-done(((bf16[4,4,16,128]{3,2,0,1:T(8,128)(2,1)}), bf16[4,4,16,128]{3,2,0,1:T(8,128)(2,1)S(1)}, u32[]{:S(2)}, u32[]{:S(2)}) %all-to-all-start) | async-done | bytes 65568 | tf_op jit(solution)/shard_map/all_to_all | solution.py:70
  21.5 3.3 %all-to-all-start.1 = ((bf16[4,4,16,128]{3,2,0,1:T(8,128)(2,1)}), bf16[4,4,16,128]{3,2,0,1:T(8,128)(2,1)S(1)}, u32[]{:S(2)}, u32[]{:S(2)}) async-start(bf16[4,4,16,128]{3,2,0,1:T(8,128)(2,1)} %get-tuple-element.48), calls=%async_computation.1 | async-start | bytes 131072 | tf_op jit(solution)/shard_map/all_to_all | solution.py:73
  24.8 0.1 broadcast_in_dim.44
  24.8 0.6 reshape.218
  25.4 0.7 pad.5.clone
  26.1 0.6 copy.31
  26.7 2.1 %all-to-all-done.1 = bf16[4,4,16,128]{3,2,0,1:T(8,128)(2,1)S(1)} async-done(((bf16[4,4,16,128]{3,2,0,1:T(8,128)(2,1)}), bf16[4,4,16,128]{3,2,0,1:T(8,128)(2,1)S(1)}, u32[]{:S(2)}, u32[]{:S(2)}) %all-to-all-start.1) | async-done | bytes 65568 | tf_op jit(solution)/shard_map/all_to_all | solution.py:73
  28.8 4.9 %all-to-all-start.2 = ((bf16[32,128,128]{2,1,0:T(8,128)(2,1)}), bf16[32,128,128]{2,1,0:T(8,128)(2,1)}, u32[]{:S(2)}, u32[]{:S(2)}) async-start(bf16[32,128,128]{2,1,0:T(8,128)(2,1)} %param.8), calls=%async_computation.2 | async-start | bytes 2097152 | tf_op jit(solution)/shard_map/all_to_all | solution.py:60
  33.7 0.6 copy.32
  34.4 0.0 collective-permute-done
  34.4 3.8 %collective-permute-start.5 = (bf16[4,128,128]{2,1,0:T(8,128)(2,1)S(1)}, bf16[4,128,128]{2,1,0:T(8,128)(2,1)S(1)}, u32[]{:S(2)}, u32[]{:S(2)}) collective-permute-start(bf16[4,128,128]{2,1,0:T(8,128)(2,1)S(1)} %get-tuple-element.29), channel_id=1, source_target_pairs={{0,6},{1,7},{2,4},{3,5},{4,2},{5,3},{6,0},{7,1},{8,14},{9,15},{10,... | collective-permute-start | bytes 393224 | tf_op jit(solution)/shard_map/ppermute | solution.py:34
  38.2 0.0 collective-permute-done.1
  38.2 1.5 %collective-permute-start.6 = (bf16[4,128,128]{2,1,0:T(8,128)(2,1)S(1)}, bf16[4,128,128]{2,1,0:T(8,128)(2,1)S(1)}, u32[]{:S(2)}, u32[]{:S(2)}) collective-permute-start(bf16[4,128,128]{2,1,0:T(8,128)(2,1)S(1)} %get-tuple-element.28), channel_id=1, source_target_pairs={{0,7},{1,6},{2,5},{3,4},{4,3},{5,2},{6,1},{7,0},{8,15},{9,14},{10,... | collective-permute-start | bytes 393224 | tf_op jit(solution)/shard_map/ppermute | solution.py:34
  39.9 18.9 %collective-permute-done.5 = bf16[4,128,128]{2,1,0:T(8,128)(2,1)S(1)} collective-permute-done((bf16[4,128,128]{2,1,0:T(8,128)(2,1)S(1)}, bf16[4,128,128]{2,1,0:T(8,128)(2,1)S(1)}, u32[]{:S(2)}, u32[]{:S(2)}) %collective-permute-start.5) | collective-permute-done | bytes 131104 | tf_op jit(solution)/shard_map/ppermute | solution.py:34
  58.8 2.3 %collective-permute-done.6 = bf16[4,128,128]{2,1,0:T(8,128)(2,1)S(1)} collective-permute-done((bf16[4,128,128]{2,1,0:T(8,128)(2,1)S(1)}, bf16[4,128,128]{2,1,0:T(8,128)(2,1)S(1)}, u32[]{:S(2)}, u32[]{:S(2)}) %collective-permute-start.6) | collective-permute-done | bytes 131104 | tf_op jit(solution)/shard_map/ppermute | solution.py:34
  61.1 0.7 gather_fusion
  61.9 0.1 copy.30
  62.0 4.2 %fusion.43 = (f32[4,1024]{1,0:T(4,128)S(1)}, f32[4,1024,192]{1,2,0:T(8,128)}) fusion(pred[4,1024,128]{1,2,0:T(32,128)(4,1)S(1)} %broadcast_compare_fusion, pred[192]{0:T(512)(128)(4,1)S(1)} %pad.5.clone, bf16[4,1024,128]{2,1,0:T(8,128)(2,1)S(1)} %bitcast.88, bf16[4,64,128]{2,1,0:T(8,128)(2,1)} %bitcast.105, bf16[4,128,128]{2,1,0:T(8,128)(2,1)S(1)} %get-tuple-element.53), kind=kOutput, calls=%fused_computation.88 | convolution fusion | flops 409731264 | bytes 4931776 | tf_op jit(solution)/shard_map/while/body/eval_jaxpr/sub | solution.py:117
  66.2 2.3 %fusion.9 = bf16[4,1024,192]{1,2,0:T(8,128)(2,1)S(1)} fusion(f32[4,1024,192]{1,2,0:T(8,128)} %get-tuple-element.51, f32[4,1024]{1,0:T(4,128)S(1)} %get-tuple-element.50), kind=kLoop, calls=%fused_computation.17 | loop fusion | flops 1572864 | bytes 4734976 | tf_op jit(solution)/shard_map/while/body/eval_jaxpr/convert_element_type | solution.py:119
  68.5 0.0 copy-start.6
  68.6 1.3 copy.33
  69.9 0.0 copy-start.1
  69.9 1.0 copy-done.1
  70.9 0.6 fusion.44
  71.4 0.7 copy.42
  72.1 3.3 %all-to-all-start.6 = ((f32[4,4,16,128]{3,2,0,1:T(8,128)}), f32[4,4,16,128]{3,2,0,1:T(8,128)S(1)}, u32[]{:S(2)}, u32[]{:S(2)}) async-start(f32[4,4,16,128]{3,2,0,1:T(8,128)} %copy.42), calls=%async_computation.6 | async-start | bytes 262144 | tf_op jit(solution)/shard_map/all_to_all | solution.py:155
  75.4 0.0 copy-start.2
  75.5 2.5 %multiply_reduce_fusion = f32[4,1024]{1,0:T(4,128)S(1)} fusion(bf16[4,1024,128]{2,1,0:T(8,128)(2,1)} %bitcast.91, bf16[4,1024,192]{1,2,0:T(8,128)(2,1)S(1)} %fusion.9, bf16[4,64,128]{2,1,0:T(8,128)(2,1)S(1)} %bitcast.107, bf16[4,128,128]{2,1,0:T(8,128)(2,1)S(1)} %get-tuple-element.52), kind=kOutput, calls=%fused_computation.12 | convolution fusion | flops 203288576 | bytes 2834432 | tf_op jit(solution)/shard_map/while/body/eval_jaxpr/irk,ikd->ird/dot_general | solution.py:120
  78.0 2.5 %fusion.1 = bf16[4,1024,192]{1,2,0:T(8,128)(2,1)S(1)} fusion(bf16[4,1024,128]{2,1,0:T(8,128)(2,1)S(1)} %bitcast.92, f32[4,1024]{1,0:T(4,128)S(1)} %multiply_reduce_fusion, f32[4,1024,192]{1,2,0:T(8,128)} %get-tuple-element.51, f32[4,1024]{1,0:T(4,128)S(1)} %get-tuple-element.50, bf16[4,64,128]{2,1,0:T(8,128)(2,1)S(1)} %bitcast.108, ...), kind=kOutput, calls=%fused_computation.5 | convolution fusion | flops 204865536 | bytes 5996544 | tf_op jit(solution)/shard_map/while/body/eval_jaxpr/ird,ikd->irk/dot_general | solution.py:124
  80.5 0.6 convolution_multiply_fusion
  81.0 0.0 copy-start.4
  81.1 0.7 copy.37
  81.7 3.3 %all-to-all-start.4 = ((f32[4,4,16,128]{3,2,0,1:T(8,128)}), f32[4,4,16,128]{3,2,0,1:T(8,128)S(1)}, u32[]{:S(2)}, u32[]{:S(2)}) async-start(f32[4,4,16,128]{3,2,0,1:T(8,128)} %copy.37), calls=%async_computation.4 | async-start | bytes 262144 | tf_op jit(solution)/shard_map/all_to_all | solution.py:154
  85.1 0.4 convolution_bitcast_fusion
  85.6 0.8 copy.45
  86.3 3.3 %all-to-all-done.4 = f32[4,4,16,128]{3,2,0,1:T(8,128)S(1)} async-done(((f32[4,4,16,128]{3,2,0,1:T(8,128)}), f32[4,4,16,128]{3,2,0,1:T(8,128)S(1)}, u32[]{:S(2)}, u32[]{:S(2)}) %all-to-all-start.4) | async-done | bytes 131104 | tf_op jit(solution)/shard_map/all_to_all | solution.py:154
  89.6 12.2 %all-to-all-start.7 = ((bf16[4,128,128]{2,0,1:T(4,128)(2,1)}), bf16[4,128,128]{2,0,1:T(4,128)(2,1)S(1)}, u32[]{:S(2)}, u32[]{:S(2)}) async-start(bf16[4,128,128]{2,0,1:T(4,128)(2,1)} %copy.45), calls=%async_computation.7 | async-start | bytes 262144 | tf_op jit(solution)/shard_map/all_to_all | solution.py:169
  101.9 0.4 convolution_bitcast_fusion.1
  102.4 0.8 copy.40
  103.2 6.1 %all-to-all-done.7 = bf16[4,128,128]{2,0,1:T(4,128)(2,1)S(1)} async-done(((bf16[4,128,128]{2,0,1:T(4,128)(2,1)}), bf16[4,128,128]{2,0,1:T(4,128)(2,1)S(1)}, u32[]{:S(2)}, u32[]{:S(2)}) %all-to-all-start.7) | async-done | bytes 131104 | tf_op jit(solution)/shard_map/all_to_all | solution.py:169
  109.2 3.4 %all-to-all-start.5 = ((bf16[4,128,128]{2,0,1:T(4,128)(2,1)}), bf16[4,128,128]{2,0,1:T(4,128)(2,1)S(1)}, u32[]{:S(2)}, u32[]{:S(2)}) async-start(bf16[4,128,128]{2,0,1:T(4,128)(2,1)} %copy.40), calls=%async_computation.5 | async-start | bytes 262144 | tf_op jit(solution)/shard_map/all_to_all | solution.py:168
  112.6 1.0 multiply_convert_fusion
  113.6 1.8 %copy.35 = bf16[4,1024,128]{2,0,1:T(4,128)(2,1)} copy(bf16[4,1024,128]{2,1,0:T(8,128)(2,1)S(1)} %multiply_convert_fusion) | data formatting | bytes 2097152 | tf_op jit(solution)/shard_map/while/body/eval_jaxpr/convert_element_type | solution.py:131
  115.4 4.5 %all-to-all-done.5 = bf16[4,128,128]{2,0,1:T(4,128)(2,1)S(1)} async-done(((bf16[4,128,128]{2,0,1:T(4,128)(2,1)}), bf16[4,128,128]{2,0,1:T(4,128)(2,1)S(1)}, u32[]{:S(2)}, u32[]{:S(2)}) %all-to-all-start.5) | async-done | bytes 131104 | tf_op jit(solution)/shard_map/all_to_all | solution.py:168
  119.9 3.6 %all-to-all-start.3 = ((bf16[4,1024,128]{2,0,1:T(4,128)(2,1)}), bf16[4,1024,128]{2,0,1:T(4,128)(2,1)S(1)}, u32[]{:S(2)}, u32[]{:S(2)}) async-start(bf16[4,1024,128]{2,0,1:T(4,128)(2,1)} %copy.35), calls=%async_computation.3 | async-start | bytes 2097152 | tf_op jit(solution)/shard_map/all_to_all | solution.py:167
  123.5 0.7 copy.46
  124.2 0.7 copy.41
  125.0 21.7 %all-to-all-done.3 = bf16[4,1024,128]{2,0,1:T(4,128)(2,1)S(1)} async-done(((bf16[4,1024,128]{2,0,1:T(4,128)(2,1)}), bf16[4,1024,128]{2,0,1:T(4,128)(2,1)S(1)}, u32[]{:S(2)}, u32[]{:S(2)}) %all-to-all-start.3) | async-done | bytes 1048608 | tf_op jit(solution)/shard_map/all_to_all | solution.py:167
  146.7 1.2 copy.36
  (35 shorter events, 0.4 us)
Async XLA Ops:
  0.6 10.3 %copy-start = (s32[4,4]{1,0:T(4,128)S(1)}, s32[4,4]{1,0:T(4,128)}, u32[]{:S(2)}) copy-start(s32[4,4]{1,0:T(4,128)} %param.11) | copy-start | bytes 196
  2.1 32.3 %collective-permute-start = (bf16[4,128,128]{2,1,0:T(8,128)(2,1)S(1)}, bf16[4,128,128]{2,1,0:T(8,128)(2,1)S(1)}, u32[]{:S(2)}, u32[]{:S(2)}) collective-permute-start(bf16[4,128,128]{2,1,0:T(8,128)(2,1)S(1)} %get-tuple-element.34), channel_id=1, source_target_pairs={{0,1},{1,0},{2,3},{3,2},{4,5},{5,4},{6,7},{7,6},{8,9},{9,8},{10,11... | collective-permute-start | bytes 393224 | tf_op jit(solution)/shard_map/ppermute | solution.py:34
  5.1 33.1 %collective-permute-start.1 = (bf16[4,128,128]{2,1,0:T(8,128)(2,1)S(1)}, bf16[4,128,128]{2,1,0:T(8,128)(2,1)S(1)}, u32[]{:S(2)}, u32[]{:S(2)}) collective-permute-start(bf16[4,128,128]{2,1,0:T(8,128)(2,1)S(1)} %get-tuple-element.33), channel_id=1, source_target_pairs={{0,2},{1,3},{2,0},{3,1},{4,6},{5,7},{6,4},{7,5},{8,10},{9,11},{10,... | collective-permute-start | bytes 393224 | tf_op jit(solution)/shard_map/ppermute | solution.py:34
  6.7 33.1 %collective-permute-start.2 = (bf16[4,128,128]{2,1,0:T(8,128)(2,1)S(1)}, bf16[4,128,128]{2,1,0:T(8,128)(2,1)S(1)}, u32[]{:S(2)}, u32[]{:S(2)}) collective-permute-start(bf16[4,128,128]{2,1,0:T(8,128)(2,1)S(1)} %get-tuple-element.32), channel_id=1, source_target_pairs={{0,3},{1,2},{2,1},{3,0},{4,7},{5,6},{6,5},{7,4},{8,11},{9,10},{10,... | collective-permute-start | bytes 393224 | tf_op jit(solution)/shard_map/ppermute | solution.py:34
  6.7 33.1 %collective-permute-start.3 = (bf16[4,128,128]{2,1,0:T(8,128)(2,1)S(1)}, bf16[4,128,128]{2,1,0:T(8,128)(2,1)S(1)}, u32[]{:S(2)}, u32[]{:S(2)}) collective-permute-start(bf16[4,128,128]{2,1,0:T(8,128)(2,1)S(1)} %get-tuple-element.31), channel_id=1, source_target_pairs={{0,4},{1,5},{2,6},{3,7},{4,0},{5,1},{6,2},{7,3},{8,12},{9,13},{10,... | collective-permute-start | bytes 393224 | tf_op jit(solution)/shard_map/ppermute | solution.py:34
  9.7 30.2 %collective-permute-start.4 = (bf16[4,128,128]{2,1,0:T(8,128)(2,1)S(1)}, bf16[4,128,128]{2,1,0:T(8,128)(2,1)S(1)}, u32[]{:S(2)}, u32[]{:S(2)}) collective-permute-start(bf16[4,128,128]{2,1,0:T(8,128)(2,1)S(1)} %get-tuple-element.30), channel_id=1, source_target_pairs={{0,5},{1,4},{2,7},{3,6},{4,1},{5,0},{6,3},{7,2},{8,13},{9,12},{10,... | collective-permute-start | bytes 393224 | tf_op jit(solution)/shard_map/ppermute | solution.py:34
  12.2 49.8 %copy-start.3 = (bf16[4,128,128]{2,1,0:T(8,128)(2,1)}, bf16[4,128,128]{2,1,0:T(8,128)(2,1)S(1)}, u32[]{:S(2)}) copy-start(bf16[4,128,128]{2,1,0:T(8,128)(2,1)S(1)} %get-tuple-element.53) | copy-start | bytes 393220
  14.1 7.4 %all-to-all-start = ((bf16[4,4,16,128]{3,2,0,1:T(8,128)(2,1)}), bf16[4,4,16,128]{3,2,0,1:T(8,128)(2,1)S(1)}, u32[]{:S(2)}, u32[]{:S(2)}) async-start(bf16[4,4,16,128]{3,2,0,1:T(8,128)(2,1)} %get-tuple-element.49), calls=%async_computation | async-start | bytes 131072 | tf_op jit(solution)/shard_map/all_to_all | solution.py:70
  21.5 7.4 %all-to-all-start.1 = ((bf16[4,4,16,128]{3,2,0,1:T(8,128)(2,1)}), bf16[4,4,16,128]{3,2,0,1:T(8,128)(2,1)S(1)}, u32[]{:S(2)}, u32[]{:S(2)}) async-start(bf16[4,4,16,128]{3,2,0,1:T(8,128)(2,1)} %get-tuple-element.48), calls=%async_computation.1 | async-start | bytes 131072 | tf_op jit(solution)/shard_map/all_to_all | solution.py:73
  28.8 39.7 %all-to-all-start.2 = ((bf16[32,128,128]{2,1,0:T(8,128)(2,1)}), bf16[32,128,128]{2,1,0:T(8,128)(2,1)}, u32[]{:S(2)}, u32[]{:S(2)}) async-start(bf16[32,128,128]{2,1,0:T(8,128)(2,1)} %param.8), calls=%async_computation.2 | async-start | bytes 2097152 | tf_op jit(solution)/shard_map/all_to_all | solution.py:60
  34.4 24.5 %collective-permute-start.5 = (bf16[4,128,128]{2,1,0:T(8,128)(2,1)S(1)}, bf16[4,128,128]{2,1,0:T(8,128)(2,1)S(1)}, u32[]{:S(2)}, u32[]{:S(2)}) collective-permute-start(bf16[4,128,128]{2,1,0:T(8,128)(2,1)S(1)} %get-tuple-element.29), channel_id=1, source_target_pairs={{0,6},{1,7},{2,4},{3,5},{4,2},{5,3},{6,0},{7,1},{8,14},{9,15},{10,... | collective-permute-start | bytes 393224 | tf_op jit(solution)/shard_map/ppermute | solution.py:34
  38.2 22.9 %collective-permute-start.6 = (bf16[4,128,128]{2,1,0:T(8,128)(2,1)S(1)}, bf16[4,128,128]{2,1,0:T(8,128)(2,1)S(1)}, u32[]{:S(2)}, u32[]{:S(2)}) collective-permute-start(bf16[4,128,128]{2,1,0:T(8,128)(2,1)S(1)} %get-tuple-element.28), channel_id=1, source_target_pairs={{0,7},{1,6},{2,5},{3,4},{4,3},{5,2},{6,1},{7,0},{8,15},{9,14},{10,... | collective-permute-start | bytes 393224 | tf_op jit(solution)/shard_map/ppermute | solution.py:34
  68.5 6.9 %copy-start.6 = (bf16[4,4,16,128]{3,2,1,0:T(8,128)(2,1)S(1)}, bf16[4,4,16,128]{3,2,1,0:T(8,128)(2,1)}, u32[]{:S(2)}) copy-start(bf16[4,4,16,128]{3,2,1,0:T(8,128)(2,1)} %copy.32) | copy-start | bytes 196612
  69.9 1.0 copy-start.1
  72.1 9.6 %all-to-all-start.6 = ((f32[4,4,16,128]{3,2,0,1:T(8,128)}), f32[4,4,16,128]{3,2,0,1:T(8,128)S(1)}, u32[]{:S(2)}, u32[]{:S(2)}) async-start(f32[4,4,16,128]{3,2,0,1:T(8,128)} %copy.42), calls=%async_computation.6 | async-start | bytes 262144 | tf_op jit(solution)/shard_map/all_to_all | solution.py:155
  75.4 2.5 %copy-start.2 = (bf16[8,4,128,128]{3,2,0,1:T(8,128)(2,1)S(1)}, bf16[8,4,128,128]{3,2,0,1:T(8,128)(2,1)}, u32[]{:S(2)}) copy-start(bf16[8,4,128,128]{3,2,0,1:T(8,128)(2,1)} %copy-done.1) | copy-start | bytes 3145732
  81.0 31.6 %copy-start.4 = (bf16[4,128,128]{2,1,0:T(8,128)(2,1)S(1)}, bf16[4,128,128]{2,1,0:T(8,128)(2,1)}, u32[]{:S(2)}) copy-start(bf16[4,128,128]{2,1,0:T(8,128)(2,1)} %copy-done.3) | copy-start | bytes 393220
  81.0 31.6 %copy-start.5 = (bf16[4,4,16,128]{3,2,1,0:T(8,128)(2,1)S(1)}, bf16[4,4,16,128]{3,2,1,0:T(8,128)(2,1)}, u32[]{:S(2)}) copy-start(bf16[4,4,16,128]{3,2,1,0:T(8,128)(2,1)} %copy.31) | copy-start | bytes 196612
  81.7 7.9 %all-to-all-start.4 = ((f32[4,4,16,128]{3,2,0,1:T(8,128)}), f32[4,4,16,128]{3,2,0,1:T(8,128)S(1)}, u32[]{:S(2)}, u32[]{:S(2)}) async-start(f32[4,4,16,128]{3,2,0,1:T(8,128)} %copy.37), calls=%async_computation.4 | async-start | bytes 262144 | tf_op jit(solution)/shard_map/all_to_all | solution.py:154
  89.6 19.6 %all-to-all-start.7 = ((bf16[4,128,128]{2,0,1:T(4,128)(2,1)}), bf16[4,128,128]{2,0,1:T(4,128)(2,1)S(1)}, u32[]{:S(2)}, u32[]{:S(2)}) async-start(bf16[4,128,128]{2,0,1:T(4,128)(2,1)} %copy.45), calls=%async_computation.7 | async-start | bytes 262144 | tf_op jit(solution)/shard_map/all_to_all | solution.py:169
  109.2 10.7 %all-to-all-start.5 = ((bf16[4,128,128]{2,0,1:T(4,128)(2,1)}), bf16[4,128,128]{2,0,1:T(4,128)(2,1)S(1)}, u32[]{:S(2)}, u32[]{:S(2)}) async-start(bf16[4,128,128]{2,0,1:T(4,128)(2,1)} %copy.40), calls=%async_computation.5 | async-start | bytes 262144 | tf_op jit(solution)/shard_map/all_to_all | solution.py:168
  119.9 26.8 %all-to-all-start.3 = ((bf16[4,1024,128]{2,0,1:T(4,128)(2,1)}), bf16[4,1024,128]{2,0,1:T(4,128)(2,1)S(1)}, u32[]{:S(2)}, u32[]{:S(2)}) async-start(bf16[4,1024,128]{2,0,1:T(4,128)(2,1)} %copy.35), calls=%async_computation.3 | async-start | bytes 2097152 | tf_op jit(solution)/shard_map/all_to_all | solution.py:167
